TPU v7x, 32 devices: a whole 2x2x4 slice. The times are simulated.
32 devices in a mesh: group: 4 (over y, core), dom: 8 (over z, x).
Axes of the slice: x: 2, y: 2, z: 4, core: 2. Of those that a mesh axis runs over, the one named last changes fastest.
Arguments:
- features: float32 [4096, 1024], P(('group', 'dom')), may hold values from -6 to 6
- known_mask: int32 [4096], P(('group', 'dom')), may hold values 0 or 1
- local_tile: bfloat16 [4096, 128], P(('group', 'dom')), may hold values from 0 to 1.5, as said below
- peer_tile: bfloat16 [4096, 256], P(('group', 'dom')), may hold values from 0 to 1.5, as said below
- cross_tile: bfloat16 [4096, 128], P(('group', 'dom')), may hold values from 0 to 1.5, as said below
- peer_rows: int32 [4, 8, 8, 32], P('group', 'dom'), may hold values from 0 to 127
- cross_rows: int32 [4, 8, 4, 32], P('group', 'dom'), may hold values from 0 to 127
- labels: int32 [4096], P(('group', 'dom')), may hold values from 0 to 18
- first_weight: bfloat16 [1024, 1024], replicated, may hold values from -0.1875 to 0.1875
- first_bias: float32 [1024], replicated, may hold values from -3 to 3
- second_weight: bfloat16 [1024, 19], replicated, may hold values from -60 to 60
- second_bias: float32 [19], replicated, may hold values from -3 to 3
Outputs:
- imputed: float32 [4096, 1024], P(('group', 'dom'))
- grad_first: float32 [1024, 1024], P('dom')
- grad_first_bias: float32 [1024], replicated
- grad_second: float32 [1024, 19], replicated
- grad_second_bias: float32 [19], replicated
Inputs may be any that keep to these rules, and one draw needn't show every extreme that they name: `local_tile`: each entry is 0 or lies in 0.5 to 1.5; a fraction of about 8 / 128 is nonzero. `peer_tile`: each entry is 0 or lies in 0.5 to 1.5; a fraction of about 6 / 256 is nonzero. `cross_tile`: each entry is 0 or lies in 0.5 to 1.5; a fraction of about 4 / 128 is nonzero.
All inputs are finite; a program needn't handle non-finite values. No bound on the sum of `known_mask` on one device may be relied on, other than what follows from the above.
Results may differ from a plain program's by a relative error of at most 0.0041.
Values sent between devices are 32-bit elements; how exact they have to be, the bound alone decides.
A program may use at most 64 MiB of HBM per device.

v0:
```python
import math
import jax
import jax.numpy as jnp
from jax import lax
from jax.sharding import PartitionSpec as P

SWEEPS = 3


def fetch_halos(current, peer_list, cross_list):
    width = current.shape[1]
    outgoing = current[peer_list.reshape(-1)].reshape(peer_list.shape[2], peer_list.shape[3], width)
    incoming = lax.all_to_all(outgoing, "dom", split_axis=0, concat_axis=0, tiled=True)
    leaving = current[cross_list.reshape(-1)].reshape(
        cross_list.shape[2], cross_list.shape[3], width
    )
    arriving = lax.all_to_all(leaving, "group", split_axis=0, concat_axis=0, tiled=True)
    return (incoming.reshape(-1, width), arriving.reshape(-1, width))


def local(
    features,
    known_mask,
    local_tile,
    peer_tile,
    cross_tile,
    peer_rows,
    cross_rows,
    labels,
    first_weight,
    first_bias,
    second_weight,
    second_bias,
):
    highest = lax.Precision.HIGHEST
    keep = (known_mask == 1)[:, None]
    current = jnp.where(keep, features, jnp.float32(0.0))
    local_full = local_tile.astype(jnp.float32)
    peer_full = peer_tile.astype(jnp.float32)
    cross_full = cross_tile.astype(jnp.float32)
    degree = (
        1.0 + jnp.sum(local_full, axis=1) + jnp.sum(peer_full, axis=1) + jnp.sum(cross_full, axis=1)
    )
    degree = degree[:, None]
    for sweep in range(SWEEPS):
        incoming, arriving = fetch_halos(current, peer_rows, cross_rows)
        summed = current + jnp.dot(
            local_full, current, precision=highest, preferred_element_type=jnp.float32
        )
        summed = summed + jnp.dot(
            peer_full, incoming, precision=highest, preferred_element_type=jnp.float32
        )
        summed = summed + jnp.dot(
            cross_full, arriving, precision=highest, preferred_element_type=jnp.float32
        )
        current = jnp.where(keep, features, summed / degree)
    inputs = current.astype(jnp.bfloat16)
    pre = jnp.dot(inputs, first_weight, preferred_element_type=jnp.float32) + first_bias
    sigma = jax.nn.sigmoid(pre)
    active = (pre * sigma).astype(jnp.bfloat16)
    logits = jnp.dot(active, second_weight, preferred_element_type=jnp.float32) + second_bias
    shifted = logits - jnp.max(logits, axis=1, keepdims=True)
    expo = jnp.exp(shifted)
    probs = expo / jnp.sum(expo, axis=1, keepdims=True)
    classes = second_weight.shape[1]
    onehot = (labels[:, None] == jnp.arange(classes, dtype=jnp.int32)[None, :]).astype(jnp.float32)
    total_nodes = features.shape[0] * lax.axis_size("group") * lax.axis_size("dom")
    dlogits = (probs - onehot) / jnp.float32(math.sqrt(total_nodes))
    dlogits_b = dlogits.astype(jnp.bfloat16)
    second_bias_term = jnp.sum(dlogits, axis=0)
    second_term = lax.dot_general(
        active, dlogits_b, (((0,), (0,)), ((), ())), preferred_element_type=jnp.float32
    )
    back = lax.dot_general(
        dlogits_b, second_weight, (((1,), (1,)), ((), ())), preferred_element_type=jnp.float32
    )
    dpre = (back * sigma * (1.0 + pre * (1.0 - sigma))).astype(jnp.bfloat16)
    first_bias_term = jnp.sum(dpre.astype(jnp.float32), axis=0)
    share = lax.psum_scatter(
        lax.dot_general(inputs, dpre, (((0,), (0,)), ((), ())), preferred_element_type=jnp.float32),
        "dom",
        scatter_dimension=0,
        tiled=True,
    )
    grad_first = lax.psum(share, "group")
    grad_first_bias, grad_second, grad_second_bias = lax.psum(
        (first_bias_term, second_term, second_bias_term), ("group", "dom")
    )
    return (current, grad_first, grad_first_bias, grad_second, grad_second_bias)


def solution(mesh):
    in_specs = (
        P(("group", "dom"), None),
        P(("group", "dom")),
        P(("group", "dom"), None),
        P(("group", "dom"), None),
        P(("group", "dom"), None),
        P("group", "dom", None, None),
        P("group", "dom", None, None),
        P(("group", "dom")),
        P(),
        P(),
        P(),
        P(),
    )
    out_specs = (P(("group", "dom"), None), P("dom", None), P(), P(), P())
    return jax.shard_map(local, mesh=mesh, in_specs=in_specs, out_specs=out_specs, check_vma=False)
```

profile of v0, /device:TPU:0, one launch (start us, length us, event | category | flops | bytes accessed | tf_op | source)
XLA Modules:
  0.0 363.8 jit_solution(1645723564046518858)
XLA Ops:
  12.3 1.6 gather_fusion.1
  13.9 4.3 %all-to-all-start.1 = ((f32[4,32,1024]{2,1,0:T(8,128)}), f32[4,32,1024]{2,1,0:T(8,128)}, u32[]{:S(2)}, u32[]{:S(2)}) async-start(f32[4,32,1024]{2,1,0:T(8,128)} %bitcast.91), calls=%async_computation.1 | async-start | bytes 1048576 | tf_op jit(solution)/shard_map/all_to_all | solution.py:17
  18.2 2.1 gather_fusion
  20.3 7.3 %all-to-all-done.1 = f32[4,32,1024]{2,1,0:T(8,128)} async-done(((f32[4,32,1024]{2,1,0:T(8,128)}), f32[4,32,1024]{2,1,0:T(8,128)}, u32[]{:S(2)}, u32[]{:S(2)}) %all-to-all-start.1) | async-done | bytes 524320 | tf_op jit(solution)/shard_map/all_to_all | solution.py:17
  27.6 6.6 %all-to-all-start = ((f32[8,32,1024]{2,1,0:T(8,128)}), f32[8,32,1024]{2,1,0:T(8,128)}, u32[]{:S(2)}, u32[]{:S(2)}) async-start(f32[8,32,1024]{2,1,0:T(8,128)} %bitcast.88), calls=%async_computation | async-start | bytes 2097152 | tf_op jit(solution)/shard_map/all_to_all | solution.py:13
  34.4 1.6 convolution_bitcast_fusion.4
  36.1 23.8 %all-to-all-done = f32[8,32,1024]{2,1,0:T(8,128)} async-done(((f32[8,32,1024]{2,1,0:T(8,128)}), f32[8,32,1024]{2,1,0:T(8,128)}, u32[]{:S(2)}, u32[]{:S(2)}) %all-to-all-start) | async-done | bytes 1048608 | tf_op jit(solution)/shard_map/all_to_all | solution.py:13
  59.9 2.2 convolution_bitcast_fusion.8
  64.6 1.6 gather_fusion.3
  66.1 4.1 %all-to-all-start.3 = ((f32[4,32,1024]{2,1,0:T(8,128)}), f32[4,32,1024]{2,1,0:T(8,128)}, u32[]{:S(2)}, u32[]{:S(2)}) async-start(f32[4,32,1024]{2,1,0:T(8,128)} %bitcast.93), calls=%async_computation.3 | async-start | bytes 1048576 | tf_op jit(solution)/shard_map/all_to_all | solution.py:17
  70.3 2.1 gather_fusion.2
  72.4 6.8 %all-to-all-done.3 = f32[4,32,1024]{2,1,0:T(8,128)} async-done(((f32[4,32,1024]{2,1,0:T(8,128)}), f32[4,32,1024]{2,1,0:T(8,128)}, u32[]{:S(2)}, u32[]{:S(2)}) %all-to-all-start.3) | async-done | bytes 524320 | tf_op jit(solution)/shard_map/all_to_all | solution.py:17
  79.2 4.4 %all-to-all-start.2 = ((f32[8,32,1024]{2,1,0:T(8,128)}), f32[8,32,1024]{2,1,0:T(8,128)}, u32[]{:S(2)}, u32[]{:S(2)}) async-start(f32[8,32,1024]{2,1,0:T(8,128)} %bitcast.90), calls=%async_computation.2 | async-start | bytes 2097152 | tf_op jit(solution)/shard_map/all_to_all | solution.py:13
  83.6 2.4 convolution_bitcast_fusion.2
  86.0 23.3 %all-to-all-done.2 = f32[8,32,1024]{2,1,0:T(8,128)} async-done(((f32[8,32,1024]{2,1,0:T(8,128)}), f32[8,32,1024]{2,1,0:T(8,128)}, u32[]{:S(2)}, u32[]{:S(2)}) %all-to-all-start.2) | async-done | bytes 1048608 | tf_op jit(solution)/shard_map/all_to_all | solution.py:13
  109.3 2.2 convolution_bitcast_fusion.7
  111.6 2.2 fusion.11
  115.0 1.6 gather_fusion.5
  116.6 4.1 %all-to-all-start.5 = ((f32[4,32,1024]{2,1,0:T(8,128)}), f32[4,32,1024]{2,1,0:T(8,128)}, u32[]{:S(2)}, u32[]{:S(2)}) async-start(f32[4,32,1024]{2,1,0:T(8,128)} %bitcast.92), calls=%async_computation.5 | async-start | bytes 1048576 | tf_op jit(solution)/shard_map/all_to_all | solution.py:17
  120.8 2.1 gather_fusion.4
  122.8 6.8 %all-to-all-done.5 = f32[4,32,1024]{2,1,0:T(8,128)} async-done(((f32[4,32,1024]{2,1,0:T(8,128)}), f32[4,32,1024]{2,1,0:T(8,128)}, u32[]{:S(2)}, u32[]{:S(2)}) %all-to-all-start.5) | async-done | bytes 524320 | tf_op jit(solution)/shard_map/all_to_all | solution.py:17
  129.6 4.2 %all-to-all-start.4 = ((f32[8,32,1024]{2,1,0:T(8,128)}), f32[8,32,1024]{2,1,0:T(8,128)}, u32[]{:S(2)}, u32[]{:S(2)}) async-start(f32[8,32,1024]{2,1,0:T(8,128)} %bitcast.89), calls=%async_computation.4 | async-start | bytes 2097152 | tf_op jit(solution)/shard_map/all_to_all | solution.py:13
  133.9 2.4 convolution_bitcast_fusion
  136.4 23.3 %all-to-all-done.4 = f32[8,32,1024]{2,1,0:T(8,128)} async-done(((f32[8,32,1024]{2,1,0:T(8,128)}), f32[8,32,1024]{2,1,0:T(8,128)}, u32[]{:S(2)}, u32[]{:S(2)}) %all-to-all-start.4) | async-done | bytes 1048608 | tf_op jit(solution)/shard_map/all_to_all | solution.py:13
  159.6 2.2 convolution_bitcast_fusion.6
  161.9 1.8 fusion.15
  165.2 2.6 fusion.17
  168.8 86.5 %reduce-scatter.2.cloned.1.call-done = f32[128,1024]{1,0:T(8,128)} async-done(((f32[1024,1024]{1,0:T(8,128)}), f32[128,1024]{1,0:T(8,128)}) %reduce-scatter.2.cloned.1.call-update) | async-done | bytes 524304 | tf_op jit(solution)/shard_map/reduce_scatter | solution.py:79
  256.5 40.4 %all-reduce = (f32[1024]{0:T(1024)}, f32[19]{0:T(128)}) all-reduce(f32[1024]{0:T(1024)S(1)} %get-tuple-element.16, f32[19]{0:T(128)S(1)} %fusion.26), channel_id=1, replica_groups=mesh['group'=4,'dom'=8] {'group','dom'}, use_global_device_ids=true, to_apply=%region_8.9 | all-reduce | flops 1043 | bytes 8344 | tf_op jit(solution)/shard_map/psum | solution.py:86
  296.8 19.7 %all-reduce.6.cloned.1.call-done = f32[1024,19]{0,1:T(8,128)} async-done(((f32[1024,19]{0,1:T(8,128)}), f32[1024,19]{0,1:T(8,128)}) %all-reduce.6.cloned.1.call-update) | async-done | bytes 77840 | tf_op jit(solution)/shard_map/psum | solution.py:86
  316.6 36.4 %all-reduce.4.cloned.1.call-done = f32[128,1024]{1,0:T(8,128)} async-done(((f32[128,1024]{1,0:T(8,128)}), f32[128,1024]{1,0:T(8,128)}) %all-reduce.4.cloned.1.call-update) | async-done | bytes 524304 | tf_op jit(solution)/shard_map/psum | solution.py:85
  353.0 1.9 copy.30
  (52 shorter events, 13.2 us)
Async XLA Ops:
  8.0 155.8 %copy-start = (bf16[1024,1024]{1,0:T(8,128)(2,1)S(1)}, bf16[1024,1024]{1,0:T(8,128)(2,1)}, u32[]{:S(2)}) copy-start(bf16[1024,1024]{1,0:T(8,128)(2,1)} %param.20) | copy-start | bytes 6291460
  8.0 4.1 %copy-start.7 = (s32[1,1,4,32]{3,2,1,0:T(4,128)S(1)}, s32[1,1,4,32]{3,2,1,0:T(4,128)}, u32[]{:S(2)}) copy-start(s32[1,1,4,32]{3,2,1,0:T(4,128)} %param.18) | copy-start | bytes 1540
  12.3 5.9 %copy-start.5 = (s32[1,1,8,32]{3,2,1,0:T(8,128)S(1)}, s32[1,1,8,32]{3,2,1,0:T(8,128)}, u32[]{:S(2)}) copy-start(s32[1,1,8,32]{3,2,1,0:T(8,128)} %param.17) | copy-start | bytes 3076
  13.9 13.7 %all-to-all-start.1 = ((f32[4,32,1024]{2,1,0:T(8,128)}), f32[4,32,1024]{2,1,0:T(8,128)}, u32[]{:S(2)}, u32[]{:S(2)}) async-start(f32[4,32,1024]{2,1,0:T(8,128)} %bitcast.91), calls=%async_computation.1 | async-start | bytes 1048576 | tf_op jit(solution)/shard_map/all_to_all | solution.py:17
  20.3 13.9 %copy-start.2 = (bf16[128,256]{1,0:T(8,128)(2,1)S(1)}, bf16[128,256]{1,0:T(8,128)(2,1)}, u32[]{:S(2)}) copy-start(bf16[128,256]{1,0:T(8,128)(2,1)} %param.15) | copy-start | bytes 196612
  20.3 14.0 %copy-start.3 = (bf16[128,128]{1,0:T(8,128)(2,1)S(1)}, bf16[128,128]{1,0:T(8,128)(2,1)}, u32[]{:S(2)}) copy-start(bf16[128,128]{1,0:T(8,128)(2,1)} %param.16) | copy-start | bytes 98308
  20.3 14.0 %copy-start.4 = (bf16[128,128]{1,0:T(8,128)(2,1)S(1)}, bf16[128,128]{1,0:T(8,128)(2,1)}, u32[]{:S(2)}) copy-start(bf16[128,128]{1,0:T(8,128)(2,1)} %param.14) | copy-start | bytes 98308
  27.6 32.3 %all-to-all-start = ((f32[8,32,1024]{2,1,0:T(8,128)}), f32[8,32,1024]{2,1,0:T(8,128)}, u32[]{:S(2)}, u32[]{:S(2)}) async-start(f32[8,32,1024]{2,1,0:T(8,128)} %bitcast.88), calls=%async_computation | async-start | bytes 2097152 | tf_op jit(solution)/shard_map/all_to_all | solution.py:13
  66.1 13.0 %all-to-all-start.3 = ((f32[4,32,1024]{2,1,0:T(8,128)}), f32[4,32,1024]{2,1,0:T(8,128)}, u32[]{:S(2)}, u32[]{:S(2)}) async-start(f32[4,32,1024]{2,1,0:T(8,128)} %bitcast.93), calls=%async_computation.3 | async-start | bytes 1048576 | tf_op jit(solution)/shard_map/all_to_all | solution.py:17
  79.2 32.4 %copy-start.1 = (f32[128,1024]{0,1:T(8,128)S(1)}, f32[128,1024]{0,1:T(8,128)}, u32[]{:S(2)}) copy-start(f32[128,1024]{0,1:T(8,128)} %fusion.7) | copy-start | bytes 1572868
  79.2 30.1 %all-to-all-start.2 = ((f32[8,32,1024]{2,1,0:T(8,128)}), f32[8,32,1024]{2,1,0:T(8,128)}, u32[]{:S(2)}, u32[]{:S(2)}) async-start(f32[8,32,1024]{2,1,0:T(8,128)} %bitcast.90), calls=%async_computation.2 | async-start | bytes 2097152 | tf_op jit(solution)/shard_map/all_to_all | solution.py:13
  116.6 13.0 %all-to-all-start.5 = ((f32[4,32,1024]{2,1,0:T(8,128)}), f32[4,32,1024]{2,1,0:T(8,128)}, u32[]{:S(2)}, u32[]{:S(2)}) async-start(f32[4,32,1024]{2,1,0:T(8,128)} %bitcast.92), calls=%async_computation.5 | async-start | bytes 1048576 | tf_op jit(solution)/shard_map/all_to_all | solution.py:17
  129.6 30.0 %all-to-all-start.4 = ((f32[8,32,1024]{2,1,0:T(8,128)}), f32[8,32,1024]{2,1,0:T(8,128)}, u32[]{:S(2)}, u32[]{:S(2)}) async-start(f32[8,32,1024]{2,1,0:T(8,128)} %bitcast.89), calls=%async_computation.4 | async-start | bytes 2097152 | tf_op jit(solution)/shard_map/all_to_all | solution.py:13
  133.9 121.4 %reduce-scatter.2.cloned.1.call-start = ((), (), s32[]{:S(2)}) async-start(), calls=%async_computation.7 | async-start | bytes 4718592 | tf_op jit(solution)/shard_map/reduce_scatter | solution.py:79
  159.6 4.1 %copy-start.9 = (f32[1024]{0:T(1024)S(1)}, f32[1024]{0:T(1024)}, u32[]{:S(2)}) copy-start(f32[1024]{0:T(1024)} %param.21) | copy-start | bytes 12292
  163.8 0.8 copy-start.8
  163.8 0.8 copy-start.10
  163.8 1.0 copy-start.6
  167.8 148.7 %all-reduce.6.cloned.1.call-start = ((), (), s32[]{:S(2)}) async-start(), calls=%async_computation.9 | async-start | bytes 196608 | tf_op jit(solution)/shard_map/psum | solution.py:86
  168.7 184.3 %all-reduce.4.cloned.1.call-start = ((), (), s32[]{:S(2)}) async-start(), calls=%async_computation.8 | async-start | bytes 1048576 | tf_op jit(solution)/shard_map/psum | solution.py:85
Sparse Core Ops, SparseCore 0:
  168.0 87.3 reduce-scatter.1
Sparse Core Ops, SparseCore 1:
  174.5 142.0 all-reduce.5
  318.8 34.2 all-reduce.3
where the time goes:
time: 365 us; the launch traced here: 364 us
  waiting for transfers between devices  234 us (64%)
  blocking collectives  40.4 us (11%)
  starting transfers between devices  27.9 us (8%)
  matrix products  23 us (6%)
  local copies, waits for them, and re-layouts  20.8 us (6%)
  between operations  15.7 us (4%)
    reduce_scatter x1, waiting for transfers between devices, local(): lax.psum_scatter(lax.dot_general(inputs, dpre, (((0,), (0,)), ((), ())),...  86.5 us
    all_to_all x3, waiting for transfers between devices, fetch_halos(): lax.all_to_all(outgoing, 'dom', split_axis=0, concat_axis=0, tiled=True)  70.4 us
    psum x1, blocking collectives, local(): lax.psum((first_bias_term, second_term, second_bias_term), ('group', 'dom'))  40.4 us
    psum x1, waiting for transfers between devices, local(): grad_first = lax.psum(share, 'group')  36.4 us
    all_to_all x3, waiting for transfers between devices, fetch_halos(): lax.all_to_all(leaving, 'group', split_axis=0, concat_axis=0, tiled=True)  20.9 us
    psum x1, waiting for transfers between devices, local(): lax.psum((first_bias_term, second_term, second_bias_term), ('group', 'dom'))  19.7 us
    all_to_all x3, starting transfers between devices, fetch_halos(): lax.all_to_all(outgoing, 'dom', split_axis=0, concat_axis=0, tiled=True)  15.2 us
    all_to_all x3, starting transfers between devices, fetch_halos(): lax.all_to_all(leaving, 'group', split_axis=0, concat_axis=0, tiled=True)  12.6 us
  transfers between devices with their start and end apart: 9, of which 9 were waited for; matrix products, arithmetic and copies ran while one was open for 4% of the time, Pallas kernels for 0%

commit v1 on v0

--- a/solution.py
+++ b/solution.py
@@ -82,7 +82,7 @@
         scatter_dimension=0,
         tiled=True,
     )
-    grad_first = lax.psum(share, "group")
+    grad_first = lax.all_gather(share, axis_name="group").sum(axis=0)
     grad_first_bias, grad_second, grad_second_bias = lax.psum(
         (first_bias_term, second_term, second_bias_term), ("group", "dom")
     )

time: 365 us -> 402 us (1.10)
  waiting for transfers between devices: 234 us -> 270 us
    psum x1, waiting for transfers between devices: 19.7 us -> 91.7 us  [local(): lax.psum((first_bias_term, second_term, second_bias_term), ('group', 'dom'))]
    psum x1 -> x0, waiting for transfers between devices: 36.4 us -> none  [local(): grad_first = lax.psum(share, 'group')]
  transfers between devices with their start and end apart: 9 -> 9, of which waited for: 9 -> 8; matrix products, arithmetic and copies ran while one was open for 4% -> 4% of each run, Pallas kernels for 0% -> 0%
where the time goes in v1:
time: 402 us; the launch traced here: 401 us
  waiting for transfers between devices  270 us (67%)
  blocking collectives  40.6 us (10%)
  starting transfers between devices  27.9 us (7%)
  matrix products  23 us (6%)
  local copies, waits for them, and re-layouts  19 us (5%)
  between operations  15.7 us (4%)
  other arithmetic  4.49 us (1%)
    psum x1, waiting for transfers between devices, local(): lax.psum((first_bias_term, second_term, second_bias_term), ('group', 'dom'))  91.7 us
    reduce_scatter x1, waiting for transfers between devices, local(): lax.psum_scatter(lax.dot_general(inputs, dpre, (((0,), (0,)), ((), ())),...  86.7 us
    all_to_all x3, waiting for transfers between devices, fetch_halos(): lax.all_to_all(outgoing, 'dom', split_axis=0, concat_axis=0, tiled=True)  70.4 us
    psum x1, blocking collectives, local(): lax.psum((first_bias_term, second_term, second_bias_term), ('group', 'dom'))  40.6 us
    all_to_all x3, waiting for transfers between devices, fetch_halos(): lax.all_to_all(leaving, 'group', split_axis=0, concat_axis=0, tiled=True)  20.9 us
    all_to_all x3, starting transfers between devices, fetch_halos(): lax.all_to_all(outgoing, 'dom', split_axis=0, concat_axis=0, tiled=True)  15.2 us
    all_to_all x3, starting transfers between devices, fetch_halos(): lax.all_to_all(leaving, 'group', split_axis=0, concat_axis=0, tiled=True)  12.6 us
  transfers between devices with their start and end apart: 9, of which 8 were waited for; matrix products, arithmetic and copies ran while one was open for 4% of the time, Pallas kernels for 0%

profile of v1, /device:TPU:0, one launch (start us, length us, event | category | flops | bytes accessed | tf_op | source)
XLA Modules:
  0.0 400.5 jit_solution(8676224123350819510)
XLA Ops:
  12.3 1.6 gather_fusion.1
  13.9 4.3 %all-to-all-start.1 = ((f32[4,32,1024]{2,1,0:T(8,128)}), f32[4,32,1024]{2,1,0:T(8,128)}, u32[]{:S(2)}, u32[]{:S(2)}) async-start(f32[4,32,1024]{2,1,0:T(8,128)} %bitcast.92), calls=%async_computation.1 | async-start | bytes 1048576 | tf_op jit(solution)/shard_map/all_to_all | solution.py:17
  18.2 2.1 gather_fusion
  20.3 7.3 %all-to-all-done.1 = f32[4,32,1024]{2,1,0:T(8,128)} async-done(((f32[4,32,1024]{2,1,0:T(8,128)}), f32[4,32,1024]{2,1,0:T(8,128)}, u32[]{:S(2)}, u32[]{:S(2)}) %all-to-all-start.1) | async-done | bytes 524320 | tf_op jit(solution)/shard_map/all_to_all | solution.py:17
  27.6 6.6 %all-to-all-start = ((f32[8,32,1024]{2,1,0:T(8,128)}), f32[8,32,1024]{2,1,0:T(8,128)}, u32[]{:S(2)}, u32[]{:S(2)}) async-start(f32[8,32,1024]{2,1,0:T(8,128)} %bitcast.89), calls=%async_computation | async-start | bytes 2097152 | tf_op jit(solution)/shard_map/all_to_all | solution.py:13
  34.4 1.6 convolution_bitcast_fusion.4
  36.1 23.8 %all-to-all-done = f32[8,32,1024]{2,1,0:T(8,128)} async-done(((f32[8,32,1024]{2,1,0:T(8,128)}), f32[8,32,1024]{2,1,0:T(8,128)}, u32[]{:S(2)}, u32[]{:S(2)}) %all-to-all-start) | async-done | bytes 1048608 | tf_op jit(solution)/shard_map/all_to_all | solution.py:13
  59.9 2.2 convolution_bitcast_fusion.8
  64.6 1.6 gather_fusion.3
  66.1 4.1 %all-to-all-start.3 = ((f32[4,32,1024]{2,1,0:T(8,128)}), f32[4,32,1024]{2,1,0:T(8,128)}, u32[]{:S(2)}, u32[]{:S(2)}) async-start(f32[4,32,1024]{2,1,0:T(8,128)} %bitcast.94), calls=%async_computation.3 | async-start | bytes 1048576 | tf_op jit(solution)/shard_map/all_to_all | solution.py:17
  70.3 2.1 gather_fusion.2
  72.4 6.8 %all-to-all-done.3 = f32[4,32,1024]{2,1,0:T(8,128)} async-done(((f32[4,32,1024]{2,1,0:T(8,128)}), f32[4,32,1024]{2,1,0:T(8,128)}, u32[]{:S(2)}, u32[]{:S(2)}) %all-to-all-start.3) | async-done | bytes 524320 | tf_op jit(solution)/shard_map/all_to_all | solution.py:17
  79.2 4.4 %all-to-all-start.2 = ((f32[8,32,1024]{2,1,0:T(8,128)}), f32[8,32,1024]{2,1,0:T(8,128)}, u32[]{:S(2)}, u32[]{:S(2)}) async-start(f32[8,32,1024]{2,1,0:T(8,128)} %bitcast.91), calls=%async_computation.2 | async-start | bytes 2097152 | tf_op jit(solution)/shard_map/all_to_all | solution.py:13
  83.6 2.4 convolution_bitcast_fusion.2
  86.0 23.3 %all-to-all-done.2 = f32[8,32,1024]{2,1,0:T(8,128)} async-done(((f32[8,32,1024]{2,1,0:T(8,128)}), f32[8,32,1024]{2,1,0:T(8,128)}, u32[]{:S(2)}, u32[]{:S(2)}) %all-to-all-start.2) | async-done | bytes 1048608 | tf_op jit(solution)/shard_map/all_to_all | solution.py:13
  109.3 2.2 convolution_bitcast_fusion.7
  111.6 2.2 fusion.11
  115.0 1.6 gather_fusion.5
  116.6 4.1 %all-to-all-start.5 = ((f32[4,32,1024]{2,1,0:T(8,128)}), f32[4,32,1024]{2,1,0:T(8,128)}, u32[]{:S(2)}, u32[]{:S(2)}) async-start(f32[4,32,1024]{2,1,0:T(8,128)} %bitcast.93), calls=%async_computation.5 | async-start | bytes 1048576 | tf_op jit(solution)/shard_map/all_to_all | solution.py:17
  120.8 2.1 gather_fusion.4
  122.8 6.8 %all-to-all-done.5 = f32[4,32,1024]{2,1,0:T(8,128)} async-done(((f32[4,32,1024]{2,1,0:T(8,128)}), f32[4,32,1024]{2,1,0:T(8,128)}, u32[]{:S(2)}, u32[]{:S(2)}) %all-to-all-start.5) | async-done | bytes 524320 | tf_op jit(solution)/shard_map/all_to_all | solution.py:17
  129.6 4.2 %all-to-all-start.4 = ((f32[8,32,1024]{2,1,0:T(8,128)}), f32[8,32,1024]{2,1,0:T(8,128)}, u32[]{:S(2)}, u32[]{:S(2)}) async-start(f32[8,32,1024]{2,1,0:T(8,128)} %bitcast.90), calls=%async_computation.4 | async-start | bytes 2097152 | tf_op jit(solution)/shard_map/all_to_all | solution.py:13
  133.9 2.4 convolution_bitcast_fusion
  136.4 23.3 %all-to-all-done.4 = f32[8,32,1024]{2,1,0:T(8,128)} async-done(((f32[8,32,1024]{2,1,0:T(8,128)}), f32[8,32,1024]{2,1,0:T(8,128)}, u32[]{:S(2)}, u32[]{:S(2)}) %all-to-all-start.4) | async-done | bytes 1048608 | tf_op jit(solution)/shard_map/all_to_all | solution.py:13
  159.6 2.2 convolution_bitcast_fusion.6
  161.9 1.8 fusion.15
  165.2 2.6 fusion.17
  167.9 86.7 %reduce-scatter.2.cloned.1.call-done = f32[128,1024]{1,0:T(8,128)} async-done(((f32[1024,1024]{1,0:T(8,128)}), f32[128,1024]{1,0:T(8,128)}) %reduce-scatter.2.cloned.1.call-update) | async-done | bytes 524304 | tf_op jit(solution)/shard_map/reduce_scatter | solution.py:79
  256.6 40.6 %all-reduce = (f32[1024]{0:T(1024)}, f32[19]{0:T(128)}) all-reduce(f32[1024]{0:T(1024)S(1)} %get-tuple-element.16, f32[19]{0:T(128)S(1)} %fusion.26), channel_id=1, replica_groups=mesh['group'=4,'dom'=8] {'group','dom'}, use_global_device_ids=true, to_apply=%region_8.9 | all-reduce | flops 1043 | bytes 8344 | tf_op jit(solution)/shard_map/psum | solution.py:86
  297.2 2.6 reduce_sum.67
  299.9 91.7 %all-reduce.3.cloned.1.call-done = f32[1024,19]{0,1:T(8,128)} async-done(((f32[1024,19]{0,1:T(8,128)}), f32[1024,19]{0,1:T(8,128)}) %all-reduce.3.cloned.1.call-update) | async-done | bytes 77840 | tf_op jit(solution)/shard_map/psum | solution.py:86
  391.6 1.5 copy.29
  (52 shorter events, 11.7 us)
Async XLA Ops:
  8.0 155.8 %copy-start = (bf16[1024,1024]{1,0:T(8,128)(2,1)S(1)}, bf16[1024,1024]{1,0:T(8,128)(2,1)}, u32[]{:S(2)}) copy-start(bf16[1024,1024]{1,0:T(8,128)(2,1)} %param.20) | copy-start | bytes 6291460
  8.0 4.1 %copy-start.7 = (s32[1,1,4,32]{3,2,1,0:T(4,128)S(1)}, s32[1,1,4,32]{3,2,1,0:T(4,128)}, u32[]{:S(2)}) copy-start(s32[1,1,4,32]{3,2,1,0:T(4,128)} %param.18) | copy-start | bytes 1540
  12.3 5.9 %copy-start.5 = (s32[1,1,8,32]{3,2,1,0:T(8,128)S(1)}, s32[1,1,8,32]{3,2,1,0:T(8,128)}, u32[]{:S(2)}) copy-start(s32[1,1,8,32]{3,2,1,0:T(8,128)} %param.17) | copy-start | bytes 3076
  13.9 13.7 %all-to-all-start.1 = ((f32[4,32,1024]{2,1,0:T(8,128)}), f32[4,32,1024]{2,1,0:T(8,128)}, u32[]{:S(2)}, u32[]{:S(2)}) async-start(f32[4,32,1024]{2,1,0:T(8,128)} %bitcast.92), calls=%async_computation.1 | async-start | bytes 1048576 | tf_op jit(solution)/shard_map/all_to_all | solution.py:17
  20.3 13.9 %copy-start.2 = (bf16[128,256]{1,0:T(8,128)(2,1)S(1)}, bf16[128,256]{1,0:T(8,128)(2,1)}, u32[]{:S(2)}) copy-start(bf16[128,256]{1,0:T(8,128)(2,1)} %param.15) | copy-start | bytes 196612
  20.3 14.0 %copy-start.3 = (bf16[128,128]{1,0:T(8,128)(2,1)S(1)}, bf16[128,128]{1,0:T(8,128)(2,1)}, u32[]{:S(2)}) copy-start(bf16[128,128]{1,0:T(8,128)(2,1)} %param.16) | copy-start | bytes 98308
  20.3 14.0 %copy-start.4 = (bf16[128,128]{1,0:T(8,128)(2,1)S(1)}, bf16[128,128]{1,0:T(8,128)(2,1)}, u32[]{:S(2)}) copy-start(bf16[128,128]{1,0:T(8,128)(2,1)} %param.14) | copy-start | bytes 98308
  27.6 32.3 %all-to-all-start = ((f32[8,32,1024]{2,1,0:T(8,128)}), f32[8,32,1024]{2,1,0:T(8,128)}, u32[]{:S(2)}, u32[]{:S(2)}) async-start(f32[8,32,1024]{2,1,0:T(8,128)} %bitcast.89), calls=%async_computation | async-start | bytes 2097152 | tf_op jit(solution)/shard_map/all_to_all | solution.py:13
  66.1 13.0 %all-to-all-start.3 = ((f32[4,32,1024]{2,1,0:T(8,128)}), f32[4,32,1024]{2,1,0:T(8,128)}, u32[]{:S(2)}, u32[]{:S(2)}) async-start(f32[4,32,1024]{2,1,0:T(8,128)} %bitcast.94), calls=%async_computation.3 | async-start | bytes 1048576 | tf_op jit(solution)/shard_map/all_to_all | solution.py:17
  79.2 32.4 %copy-start.1 = (f32[128,1024]{0,1:T(8,128)S(1)}, f32[128,1024]{0,1:T(8,128)}, u32[]{:S(2)}) copy-start(f32[128,1024]{0,1:T(8,128)} %fusion.7) | copy-start | bytes 1572868
  79.2 30.1 %all-to-all-start.2 = ((f32[8,32,1024]{2,1,0:T(8,128)}), f32[8,32,1024]{2,1,0:T(8,128)}, u32[]{:S(2)}, u32[]{:S(2)}) async-start(f32[8,32,1024]{2,1,0:T(8,128)} %bitcast.91), calls=%async_computation.2 | async-start | bytes 2097152 | tf_op jit(solution)/shard_map/all_to_all | solution.py:13
  116.6 13.0 %all-to-all-start.5 = ((f32[4,32,1024]{2,1,0:T(8,128)}), f32[4,32,1024]{2,1,0:T(8,128)}, u32[]{:S(2)}, u32[]{:S(2)}) async-start(f32[4,32,1024]{2,1,0:T(8,128)} %bitcast.93), calls=%async_computation.5 | async-start | bytes 1048576 | tf_op jit(solution)/shard_map/all_to_all | solution.py:17
  129.6 30.0 %all-to-all-start.4 = ((f32[8,32,1024]{2,1,0:T(8,128)}), f32[8,32,1024]{2,1,0:T(8,128)}, u32[]{:S(2)}, u32[]{:S(2)}) async-start(f32[8,32,1024]{2,1,0:T(8,128)} %bitcast.90), calls=%async_computation.4 | async-start | bytes 2097152 | tf_op jit(solution)/shard_map/all_to_all | solution.py:13
  133.9 120.7 %reduce-scatter.2.cloned.1.call-start = ((), (), s32[]{:S(2)}) async-start(), calls=%async_computation.7 | async-start | bytes 4718592 | tf_op jit(solution)/shard_map/reduce_scatter | solution.py:79
  159.6 4.1 %copy-start.9 = (f32[1024]{0:T(1024)S(1)}, f32[1024]{0:T(1024)}, u32[]{:S(2)}) copy-start(f32[1024]{0:T(1024)} %param.21) | copy-start | bytes 12292
  163.8 0.8 copy-start.8
  163.8 0.8 copy-start.10
  163.8 1.0 copy-start.6
  167.8 129.4 %all-gather.3.cloned.1.call-start = ((), (), s32[]{:S(2)}) async-start(), calls=%async_computation.9 | async-start | bytes 2621440 | tf_op jit(solution)/shard_map/all_gather | solution.py:85
  254.6 136.9 %all-reduce.3.cloned.1.call-start = ((), (), s32[]{:S(2)}) async-start(), calls=%async_computation.8 | async-start | bytes 196608 | tf_op jit(solution)/shard_map/psum | solution.py:86
Sparse Core Ops, SparseCore 0:
  168.0 86.5 reduce-scatter.1
  256.1 22.4 all-gather.2
Sparse Core Ops, SparseCore 1:
  261.3 130.2 all-reduce.2
